TPU v7x, 32 devices: a whole 2x2x4 slice. The times are simulated.
32 devices in a mesh: tm: 8 (over z, y), space: 4 (over x, core).
Axes of the slice: x: 2, y: 2, z: 4, core: 2. Of those that a mesh axis runs over, the one named last changes fastest.
Arguments:
- controls: bfloat16 [32, 64, 2048], P('tm', None, 'space'), may hold values from -4 to 4
- target: bfloat16 [64, 2048], P(None, 'space'), may hold values from -4 to 4
- state_in: float32 [8, 64, 2048], P('tm', None, 'space'), may hold values from -2.5 to 2.5
- adjoint_in: float32 [8, 64, 2048], P('tm', None, 'space'), may hold values from -5 to 5
- block_inverse: bfloat16 [64, 64, 2048], P(None, None, 'space'), may hold values from -1 to 1
- numbering: int32 [4, 512], P('space'), may hold values from 0 to 511, each once within a row
Outputs:
- new_controls: bfloat16 [32, 64, 2048], P('tm', None, 'space')
- next_state: float32 [8, 64, 2048], P('tm', None, 'space')
- next_adjoint: float32 [8, 64, 2048], P('tm', None, 'space')
- objective: float32 [], replicated
Inputs may be any that keep to these rules, and one draw needn't show every extreme that they name: `numbering`: each row names every structural element of its slab exactly once.
All inputs are finite; a program needn't handle non-finite values.
Results may differ from a plain program's by a relative error of at most 0.0085.
Values may be sent and summed in bfloat16 or wider, within the bound.
A program may use at most 128 MiB of HBM per device.

v0:
```python
import jax
import jax.numpy as jnp
from jax import lax
from jax.sharding import PartitionSpec as P

NSIDE = 4
EXY = 16


TIME_STEP = 0.1
PENALTY = 0.5
REGULAR = 0.1


def padded_2(cells, sides, width):
    for axis, dim in sides:
        count = lax.axis_size(axis)
        ends = count - 1
        head = lax.slice_in_dim(cells, 0, width, axis=dim)
        tail = lax.slice_in_dim(cells, cells.shape[dim] - width, cells.shape[dim], axis=dim)
        cells = jnp.concatenate(
            [
                lax.ppermute(tail, axis, [(i, (i + 1) % count) for i in range(ends)]),
                cells,
                lax.ppermute(head, axis, [((i + 1) % count, i) for i in range(ends)]),
            ],
            axis=dim,
        )
    return cells


def from_behind(shard, axis, by):
    length = lax.axis_size(axis)
    pairs = [(i, i + by) for i in range(length) if 0 <= i + by < length]
    return lax.ppermute(shard, axis, pairs)


def apply_block(blocks, right_side):
    return jnp.einsum("ije,je->ie", blocks, right_side, preferred_element_type=jnp.float32)


def apply_transpose(blocks, vector):
    return jnp.einsum("ije,ie->je", blocks, vector, preferred_element_type=jnp.float32)


def face_jumps(values, fetch, edges, node_side, elements):
    tensor = values.reshape(node_side, node_side, node_side, elements)
    last = node_side - 1
    lower_rim, upper_rim = edges(tensor[0], tensor[last])
    padded = padded_2(
        jnp.stack([lower_rim, upper_rim]).astype(jnp.bfloat16), (("space", 0),), 1
    ).astype(jnp.float32)
    rims = (padded[0], padded[3])
    west_jump = fetch("west", tensor[:, :, last, :], rims) - tensor[:, :, 0, :]
    east_jump = fetch("east", tensor[:, :, 0, :], rims) - tensor[:, :, last, :]
    south_jump = fetch("south", tensor[:, last, :, :], rims) - tensor[:, 0, :, :]
    north_jump = fetch("north", tensor[:, 0, :, :], rims) - tensor[:, last, :, :]
    lower_jump = fetch("lower", tensor[last], rims) - tensor[0]
    upper_jump = fetch("upper", tensor[0], rims) - tensor[last]
    total = jnp.zeros_like(tensor)
    total = total.at[:, :, 0, :].add(west_jump)
    total = total.at[:, :, last, :].add(east_jump)
    total = total.at[:, 0, :, :].add(south_jump)
    total = total.at[:, last, :, :].add(north_jump)
    total = total.at[0].add(lower_jump)
    total = total.at[last].add(upper_jump)
    return total.reshape(values.shape)


def per_device(controls, target, state_in, adjoint_in, block_inverse, numbering):
    steps_here = controls.shape[0]
    nodes = controls.shape[1]
    elements = controls.shape[2]
    node_side = NSIDE
    layer_cells = EXY * EXY
    layers = elements // layer_cells
    ordering = numbering[0]
    position = jnp.arange(elements, dtype=jnp.int32)
    inverse = jnp.zeros((elements,), jnp.int32).at[ordering].set(position)

    def arrange(values):
        return jnp.take(values, inverse, axis=-1)

    def restore(values):
        return jnp.take(values, ordering, axis=-1)

    def edges(lower_face, upper_face):
        return (lower_face[:, :, :layer_cells], upper_face[:, :, elements - layer_cells :])

    def fetch(face_name, traces, rims):
        shaped = traces.reshape(node_side, node_side, layers, EXY, EXY)
        if face_name == "west":
            moved = jnp.roll(shaped, 1, axis=4)
        elif face_name == "east":
            moved = jnp.roll(shaped, -1, axis=4)
        elif face_name == "south":
            moved = jnp.roll(shaped, 1, axis=3)
        elif face_name == "north":
            moved = jnp.roll(shaped, -1, axis=3)
        elif face_name == "lower":
            remote = rims[0].reshape(node_side, node_side, 1, EXY, EXY)
            moved = jnp.concatenate([remote, shaped[:, :, :-1]], axis=2)
        else:
            remote = rims[1].reshape(node_side, node_side, 1, EXY, EXY)
            moved = jnp.concatenate([shaped[:, :, 1:], remote], axis=2)
        return moved.reshape(traces.shape)

    def jumps_of(values):
        return face_jumps(values, fetch, edges, node_side, elements)

    blocks = arrange(block_inverse)
    goal = arrange(target).astype(jnp.float32)
    controls_here = arrange(controls)
    start_state = arrange(state_in[0])
    start_adjoint = arrange(adjoint_in[0])
    total_steps = steps_here * lax.axis_size("tm")
    first_step = lax.axis_index("tm") * steps_here
    history = [start_state]
    state = start_state
    misfit = jnp.float32(0.0)
    regular_sum = jnp.float32(0.0)
    right_side = None
    for index_k in range(steps_here):
        control_now = controls_here[index_k].astype(jnp.float32)
        right_side = (
            state
            + TIME_STEP * (state - state * state * state)
            + TIME_STEP * PENALTY * jumps_of(state)
            + TIME_STEP * control_now
        ).astype(jnp.bfloat16)
        state = apply_block(blocks, right_side)
        history.append(state)
        weight = (first_step + index_k + 1).astype(jnp.float32) / total_steps
        misfit = misfit + weight * jnp.sum((state - goal) ** 2)
        regular_sum = regular_sum + jnp.sum(control_now * control_now)
    local_cost = 0.5 * misfit + 0.5 * REGULAR * regular_sum
    end_weight = (first_step + steps_here).astype(jnp.float32) / total_steps
    adjoint = end_weight * (history[-1] - goal) + start_adjoint
    updated = [None] * steps_here
    carried = adjoint
    for index_k in reversed(range(steps_here)):
        pulled = apply_transpose(blocks, adjoint.astype(jnp.bfloat16))
        control_now = controls_here[index_k].astype(jnp.float32)
        updated[index_k] = (control_now - (TIME_STEP * pulled + REGULAR * control_now)).astype(
            jnp.bfloat16
        )
        before = history[index_k]
        carried = (
            pulled
            + TIME_STEP * (1.0 - 3.0 * before * before) * pulled
            + TIME_STEP * PENALTY * jumps_of(pulled)
        )
        if index_k > 0:
            weight = (first_step + index_k).astype(jnp.float32) / total_steps
            adjoint = weight * (before - goal) + carried
    new_controls = restore(jnp.stack(updated))
    objective = lax.psum(local_cost, ("tm", "space")) / (
        total_steps * nodes * elements * lax.axis_size("space")
    )
    moved_state = from_behind(history[-1].astype(jnp.bfloat16), "tm", 1).astype(jnp.float32)
    next_state = jnp.where(lax.axis_index("tm") == 0, state_in[0], restore(moved_state))[None]
    next_adjoint = from_behind(restore(carried), "tm", -1)[None]
    return (new_controls, next_state, next_adjoint, objective)


def solution(mesh):
    return jax.shard_map(
        per_device,
        mesh=mesh,
        in_specs=(
            P("tm", None, "space"),
            P(None, "space"),
            P("tm", None, "space"),
            P("tm", None, "space"),
            P(None, None, "space"),
            P("space", None),
        ),
        out_specs=(P("tm", None, "space"), P("tm", None, "space"), P("tm", None, "space"), P()),
        check_vma=False,
    )
```

profile of v0, /device:TPU:0, one launch (start us, length us, event | category | flops | bytes accessed | tf_op | source)
XLA Modules:
  0.0 265.1 jit_solution(15748085955801050513)
XLA Ops:
  1.4 2.4 scatter_custom_fusion
  3.9 1.0 copy.142
  4.9 1.0 gather_fusion.3
  6.1 2.4 collective-permute-start
  8.6 1.3 collective-permute-start.1
  13.3 2.1 gather_fusion.2
  16.1 13.0 %copy.148 = bf16[64,64,512]{1,0,2:T(8,128)(2,1)} copy(bf16[64,64,512]{2,1,0:T(8,128)(2,1)} %param.110) | data formatting | bytes 8388608 | tf_op args[4]
  29.1 23.0 %gather_fusion = bf16[512,64,64]{2,1,0:T(8,128)(2,1)} fusion(bf16[64,64,512]{1,0,2:T(8,128)(2,1)} %copy.148, s32[1024]{0:T(1024)S(1)} %pad_clamp_fusion.1), kind=kCustom, calls=%fused_computation.6 | custom fusion | bytes 8390656 | tf_op jit(solution)/shard_map/jit(_take)/gather | solution.py:82
  52.3 1.3 gather_fusion.1
  53.9 1.0 gather_fusion.4
  56.1 8.3 %fusion = f32[512,64]{1,0:T(8,128)S(1)} fusion(f32[512,64]{1,0:T(8,128)S(1)} %copy.235, bf16[512,64,64]{2,1,0:T(8,128)(2,1)} %gather_fusion, pred[512]{0:T(512)(128)(4,1)S(1)} %compare_and_fusion.1), kind=kLoop, calls=%fused_computation.17 | loop fusion | flops 8355840 | bytes 4456960
  66.8 5.1 %collective-permute-start.2 = (bf16[1,4,4,256]{3,2,1,0:T(4,128)(2,1)S(1)}, bf16[1,4,4,256]{3,2,1,0:T(4,128)(2,1)S(1)}, u32[]{:S(2)}, u32[]{:S(2)}) collective-permute-start(bf16[1,4,4,256]{3,2,1,0:T(4,128)(2,1)S(1)} %slice_bitcast_fusion.17), channel_id=1, source_target_pairs={{0,1},{1,2},{2,3},{4,5},{5,6},{6,7},{8,9},{9,10},{10,11},{12,13},{... | collective-permute-start | bytes 24584 | tf_op jit(solution)/shard_map/ppermute | solution.py:23
  72.0 1.3 collective-permute-start.3
  73.8 2.4 collective-permute-done.3
  77.2 8.1 %fusion.1 = f32[512,64]{1,0:T(8,128)S(1)} fusion(f32[512,64]{1,0:T(8,128)S(1)} %copy.236, bf16[512,64,64]{2,1,0:T(8,128)(2,1)} %gather_fusion, pred[512]{0:T(512)(128)(4,1)S(1)} %compare_and_fusion.1), kind=kLoop, calls=%fused_computation.18 | loop fusion | flops 8355840 | bytes 4456960
  87.8 4.3 %collective-permute-start.4 = (bf16[1,4,4,256]{3,2,1,0:T(4,128)(2,1)S(1)}, bf16[1,4,4,256]{3,2,1,0:T(4,128)(2,1)S(1)}, u32[]{:S(2)}, u32[]{:S(2)}) collective-permute-start(bf16[1,4,4,256]{3,2,1,0:T(4,128)(2,1)S(1)} %slice_bitcast_fusion.15), channel_id=1, source_target_pairs={{0,1},{1,2},{2,3},{4,5},{5,6},{6,7},{8,9},{9,10},{10,11},{12,13},{... | collective-permute-start | bytes 24584 | tf_op jit(solution)/shard_map/ppermute | solution.py:23
  92.1 1.3 collective-permute-start.5
  94.0 1.2 collective-permute-done.5
  96.1 8.3 %fusion.2 = f32[512,64]{1,0:T(8,128)S(1)} fusion(f32[512,64]{1,0:T(8,128)S(1)} %copy.237, bf16[512,64,64]{2,1,0:T(8,128)(2,1)} %gather_fusion, pred[512]{0:T(512)(128)(4,1)S(1)} %compare_and_fusion.1), kind=kLoop, calls=%fused_computation.19 | loop fusion | flops 8355840 | bytes 4456960
  106.9 3.8 %collective-permute-start.6 = (bf16[1,4,4,256]{3,2,1,0:T(4,128)(2,1)S(1)}, bf16[1,4,4,256]{3,2,1,0:T(4,128)(2,1)S(1)}, u32[]{:S(2)}, u32[]{:S(2)}) collective-permute-start(bf16[1,4,4,256]{3,2,1,0:T(4,128)(2,1)S(1)} %slice_bitcast_fusion.13), channel_id=1, source_target_pairs={{0,1},{1,2},{2,3},{4,5},{5,6},{6,7},{8,9},{9,10},{10,11},{12,13},{... | collective-permute-start | bytes 24584 | tf_op jit(solution)/shard_map/ppermute | solution.py:23
  110.8 1.3 collective-permute-start.7
  112.7 1.2 collective-permute-done.7
  114.8 8.1 %fusion.3 = f32[512,64]{1,0:T(8,128)S(1)} fusion(f32[512,64]{1,0:T(8,128)S(1)} %copy.238, bf16[512,64,64]{2,1,0:T(8,128)(2,1)} %gather_fusion, pred[512]{0:T(512)(128)(4,1)S(1)} %compare_and_fusion.1), kind=kLoop, calls=%fused_computation.20 | loop fusion | flops 8355840 | bytes 4456960
  123.2 8.2 %fusion.4 = f32[512,64]{1,0:T(8,128)S(1)} fusion(f32[512,64]{1,0:T(8,128)S(1)} %copy.239, bf16[512,64,64]{2,1,0:T(8,128)(2,1)} %gather_fusion, pred[512]{0:T(512)(128)(4,1)S(1)} %compare_and_fusion.1), kind=kLoop, calls=%fused_computation.21 | loop fusion | flops 8355840 | bytes 4456960
  134.1 3.8 %collective-permute-start.8 = (bf16[1,4,4,256]{3,2,1,0:T(4,128)(2,1)S(1)}, bf16[1,4,4,256]{3,2,1,0:T(4,128)(2,1)S(1)}, u32[]{:S(2)}, u32[]{:S(2)}) collective-permute-start(bf16[1,4,4,256]{3,2,1,0:T(4,128)(2,1)S(1)} %slice_bitcast_fusion.11), channel_id=1, source_target_pairs={{0,1},{1,2},{2,3},{4,5},{5,6},{6,7},{8,9},{9,10},{10,11},{12,13},{... | collective-permute-start | bytes 24584 | tf_op jit(solution)/shard_map/ppermute | solution.py:23
  138.0 1.3 collective-permute-start.9
  139.5 3.4 %collective-permute-start.14 = (bf16[64,512]{1,0:T(8,128)(2,1)S(1)}, bf16[64,512]{1,0:T(8,128)(2,1)S(1)}, u32[]{:S(2)}, u32[]{:S(2)}) collective-permute-start(bf16[64,512]{1,0:T(8,128)(2,1)S(1)} %bitcast_convert_fusion), channel_id=1, source_target_pairs={{0,4},{4,8},{8,12},{12,16},{16,20},{20,24},{24,28},{1,5},{5,9},{9,... | collective-permute-start | bytes 196616 | tf_op jit(solution)/shard_map/ppermute | solution.py:35
  144.1 8.6 %fusion.5 = f32[512,64]{1,0:T(8,128)S(1)} fusion(f32[512,64]{1,0:T(8,128)S(1)} %copy.240, bf16[512,64,64]{2,1,0:T(8,128)(2,1)} %gather_fusion, pred[512]{0:T(512)(128)(4,1)S(1)} %compare_and_fusion.1), kind=kLoop, calls=%fused_computation.22 | loop fusion | flops 8355840 | bytes 4456960
  155.2 2.8 %collective-permute-start.10 = (bf16[1,4,4,256]{3,2,1,0:T(4,128)(2,1)S(1)}, bf16[1,4,4,256]{3,2,1,0:T(4,128)(2,1)S(1)}, u32[]{:S(2)}, u32[]{:S(2)}) collective-permute-start(bf16[1,4,4,256]{3,2,1,0:T(4,128)(2,1)S(1)} %slice_bitcast_fusion.9), channel_id=1, source_target_pairs={{0,1},{1,2},{2,3},{4,5},{5,6},{6,7},{8,9},{9,10},{10,11},{12,13},{... | collective-permute-start | bytes 24584 | tf_op jit(solution)/shard_map/ppermute | solution.py:23
  158.0 1.3 collective-permute-start.11
  159.9 2.2 collective-permute-done.11
  163.7 8.2 %fusion.6 = f32[512,64]{1,0:T(8,128)S(1)} fusion(f32[512,64]{1,0:T(8,128)S(1)} %copy.241, bf16[512,64,64]{2,1,0:T(8,128)(2,1)} %gather_fusion, pred[512]{0:T(512)(128)(4,1)S(1)} %compare_and_fusion.1), kind=kLoop, calls=%fused_computation.23 | loop fusion | flops 8355840 | bytes 4456960
  174.4 4.3 %collective-permute-start.12 = (bf16[1,4,4,256]{3,2,1,0:T(4,128)(2,1)S(1)}, bf16[1,4,4,256]{3,2,1,0:T(4,128)(2,1)S(1)}, u32[]{:S(2)}, u32[]{:S(2)}) collective-permute-start(bf16[1,4,4,256]{3,2,1,0:T(4,128)(2,1)S(1)} %slice_bitcast_fusion.7), channel_id=1, source_target_pairs={{0,1},{1,2},{2,3},{4,5},{5,6},{6,7},{8,9},{9,10},{10,11},{12,13},{... | collective-permute-start | bytes 24584 | tf_op jit(solution)/shard_map/ppermute | solution.py:23
  178.7 1.3 collective-permute-start.13
  184.2 8.2 %fusion.7 = f32[512,64]{1,0:T(8,128)S(1)} fusion(f32[512,64]{1,0:T(8,128)S(1)} %copy.242, bf16[512,64,64]{2,1,0:T(8,128)(2,1)} %gather_fusion, pred[512]{0:T(512)(128)(4,1)S(1)} %compare_and_fusion.1), kind=kLoop, calls=%fused_computation.24 | loop fusion | flops 8355840 | bytes 4456960
  194.8 3.0 %collective-permute-start.15 = (bf16[1,4,4,256]{3,2,1,0:T(4,128)(2,1)S(1)}, bf16[1,4,4,256]{3,2,1,0:T(4,128)(2,1)S(1)}, u32[]{:S(2)}, u32[]{:S(2)}) collective-permute-start(bf16[1,4,4,256]{3,2,1,0:T(4,128)(2,1)S(1)} %slice_bitcast_fusion.5), channel_id=1, source_target_pairs={{0,1},{1,2},{2,3},{4,5},{5,6},{6,7},{8,9},{9,10},{10,11},{12,13},{... | collective-permute-start | bytes 24584 | tf_op jit(solution)/shard_map/ppermute | solution.py:23
  197.9 1.5 collective-permute-start.16
  200.0 1.8 collective-permute-done.16
  203.7 2.1 gather_fusion.5
  205.8 1.0 gather_fusion.7
  209.4 1.8 select_bitcast_fusion
  211.3 41.3 %psum.7 = f32[]{:T(128)} all-reduce(f32[]{:T(128)S(6)} %add.563), channel_id=1, replica_groups=mesh['tm'=8,'space'=4] {'tm','space'}, use_global_device_ids=true, to_apply=%region_9.12 | all-reduce | flops 1 | bytes 8 | tf_op jit(solution)/shard_map/psum | solution.py:157
  252.7 1.0 copy.184
  253.7 1.3 collective-permute-start.17
  255.7 1.0 gather_fusion.6
  256.9 0.8 copy.185
  257.7 5.3 %collective-permute-done.17 = f32[64,512]{0,1:T(8,128)S(1)} collective-permute-done((f32[64,512]{0,1:T(8,128)S(1)}, f32[64,512]{0,1:T(8,128)S(1)}, u32[]{:S(2)}, u32[]{:S(2)}) %collective-permute-start.17) | collective-permute-done | bytes 131104 | tf_op jit(solution)/shard_map/ppermute | solution.py:35
  263.0 0.8 copy.186
  (453 shorter events, 34.2 us)
Async XLA Ops:
  0.6 12.1 %copy-start.3 = (s32[1,512]{1,0:T(1,128)S(1)}, s32[1,512]{1,0:T(1,128)}, u32[]{:S(2)}) copy-start(s32[1,512]{1,0:T(1,128)} %param.111) | copy-start | bytes 6148
  0.6 12.3 %copy-start = (bf16[4,64,512]{2,1,0:T(8,128)(2,1)S(1)}, bf16[4,64,512]{2,1,0:T(8,128)(2,1)}, u32[]{:S(2)}) copy-start(bf16[4,64,512]{2,1,0:T(8,128)(2,1)} %param.106) | copy-start | bytes 786436
  6.1 48.9 %collective-permute-start = (bf16[1,4,4,256]{3,2,1,0:T(4,128)(2,1)S(1)}, bf16[1,4,4,256]{3,2,1,0:T(4,128)(2,1)S(1)}, u32[]{:S(2)}, u32[]{:S(2)}) collective-permute-start(bf16[1,4,4,256]{3,2,1,0:T(4,128)(2,1)S(1)} %slice_bitcast_fusion.19), channel_id=1, source_target_pairs={{0,1},{1,2},{2,3},{4,5},{5,6},{6,7},{8,9},{9,10},{10,11},{12,13},{... | collective-permute-start | bytes 24584 | tf_op jit(solution)/shard_map/ppermute | solution.py:23
  8.6 46.5 %collective-permute-start.1 = (bf16[1,4,4,256]{3,2,1,0:T(4,128)(2,1)S(1)}, bf16[1,4,4,256]{3,2,1,0:T(4,128)(2,1)S(1)}, u32[]{:S(2)}, u32[]{:S(2)}) collective-permute-start(bf16[1,4,4,256]{3,2,1,0:T(4,128)(2,1)S(1)} %slice_bitcast_fusion.18), channel_id=1, source_target_pairs={{1,0},{2,1},{3,2},{5,4},{6,5},{7,6},{9,8},{10,9},{11,10},{13,12},{... | collective-permute-start | bytes 24584 | tf_op jit(solution)/shard_map/ppermute | solution.py:25
  16.1 36.1 %copy-start.2 = (bf16[64,512]{1,0:T(8,128)(2,1)S(1)}, bf16[64,512]{1,0:T(8,128)(2,1)}, u32[]{:S(2)}) copy-start(bf16[64,512]{1,0:T(8,128)(2,1)} %param.107) | copy-start | bytes 196612
  16.1 37.7 %copy-start.1 = (f32[1,64,512]{2,1,0:T(8,128)S(1)}, f32[1,64,512]{2,1,0:T(8,128)}, u32[]{:S(2)}) copy-start(f32[1,64,512]{2,1,0:T(8,128)} %param.109) | copy-start | bytes 393220
  66.8 7.1 %collective-permute-start.2 = (bf16[1,4,4,256]{3,2,1,0:T(4,128)(2,1)S(1)}, bf16[1,4,4,256]{3,2,1,0:T(4,128)(2,1)S(1)}, u32[]{:S(2)}, u32[]{:S(2)}) collective-permute-start(bf16[1,4,4,256]{3,2,1,0:T(4,128)(2,1)S(1)} %slice_bitcast_fusion.17), channel_id=1, source_target_pairs={{0,1},{1,2},{2,3},{4,5},{5,6},{6,7},{8,9},{9,10},{10,11},{12,13},{... | collective-permute-start | bytes 24584 | tf_op jit(solution)/shard_map/ppermute | solution.py:23
  72.0 4.3 %collective-permute-start.3 = (bf16[1,4,4,256]{3,2,1,0:T(4,128)(2,1)S(1)}, bf16[1,4,4,256]{3,2,1,0:T(4,128)(2,1)S(1)}, u32[]{:S(2)}, u32[]{:S(2)}) collective-permute-start(bf16[1,4,4,256]{3,2,1,0:T(4,128)(2,1)S(1)} %slice_bitcast_fusion.16), channel_id=1, source_target_pairs={{1,0},{2,1},{3,2},{5,4},{6,5},{7,6},{9,8},{10,9},{11,10},{13,12},{... | collective-permute-start | bytes 24584 | tf_op jit(solution)/shard_map/ppermute | solution.py:25
  87.8 6.2 %collective-permute-start.4 = (bf16[1,4,4,256]{3,2,1,0:T(4,128)(2,1)S(1)}, bf16[1,4,4,256]{3,2,1,0:T(4,128)(2,1)S(1)}, u32[]{:S(2)}, u32[]{:S(2)}) collective-permute-start(bf16[1,4,4,256]{3,2,1,0:T(4,128)(2,1)S(1)} %slice_bitcast_fusion.15), channel_id=1, source_target_pairs={{0,1},{1,2},{2,3},{4,5},{5,6},{6,7},{8,9},{9,10},{10,11},{12,13},{... | collective-permute-start | bytes 24584 | tf_op jit(solution)/shard_map/ppermute | solution.py:23
  92.1 3.1 %collective-permute-start.5 = (bf16[1,4,4,256]{3,2,1,0:T(4,128)(2,1)S(1)}, bf16[1,4,4,256]{3,2,1,0:T(4,128)(2,1)S(1)}, u32[]{:S(2)}, u32[]{:S(2)}) collective-permute-start(bf16[1,4,4,256]{3,2,1,0:T(4,128)(2,1)S(1)} %slice_bitcast_fusion.14), channel_id=1, source_target_pairs={{1,0},{2,1},{3,2},{5,4},{6,5},{7,6},{9,8},{10,9},{11,10},{13,12},{... | collective-permute-start | bytes 24584 | tf_op jit(solution)/shard_map/ppermute | solution.py:25
  106.9 5.8 %collective-permute-start.6 = (bf16[1,4,4,256]{3,2,1,0:T(4,128)(2,1)S(1)}, bf16[1,4,4,256]{3,2,1,0:T(4,128)(2,1)S(1)}, u32[]{:S(2)}, u32[]{:S(2)}) collective-permute-start(bf16[1,4,4,256]{3,2,1,0:T(4,128)(2,1)S(1)} %slice_bitcast_fusion.13), channel_id=1, source_target_pairs={{0,1},{1,2},{2,3},{4,5},{5,6},{6,7},{8,9},{9,10},{10,11},{12,13},{... | collective-permute-start | bytes 24584 | tf_op jit(solution)/shard_map/ppermute | solution.py:23
  110.8 3.1 %collective-permute-start.7 = (bf16[1,4,4,256]{3,2,1,0:T(4,128)(2,1)S(1)}, bf16[1,4,4,256]{3,2,1,0:T(4,128)(2,1)S(1)}, u32[]{:S(2)}, u32[]{:S(2)}) collective-permute-start(bf16[1,4,4,256]{3,2,1,0:T(4,128)(2,1)S(1)} %slice_bitcast_fusion.12), channel_id=1, source_target_pairs={{1,0},{2,1},{3,2},{5,4},{6,5},{7,6},{9,8},{10,9},{11,10},{13,12},{... | collective-permute-start | bytes 24584 | tf_op jit(solution)/shard_map/ppermute | solution.py:25
  134.1 9.0 %collective-permute-start.8 = (bf16[1,4,4,256]{3,2,1,0:T(4,128)(2,1)S(1)}, bf16[1,4,4,256]{3,2,1,0:T(4,128)(2,1)S(1)}, u32[]{:S(2)}, u32[]{:S(2)}) collective-permute-start(bf16[1,4,4,256]{3,2,1,0:T(4,128)(2,1)S(1)} %slice_bitcast_fusion.11), channel_id=1, source_target_pairs={{0,1},{1,2},{2,3},{4,5},{5,6},{6,7},{8,9},{9,10},{10,11},{12,13},{... | collective-permute-start | bytes 24584 | tf_op jit(solution)/shard_map/ppermute | solution.py:23
  138.0 5.2 %collective-permute-start.9 = (bf16[1,4,4,256]{3,2,1,0:T(4,128)(2,1)S(1)}, bf16[1,4,4,256]{3,2,1,0:T(4,128)(2,1)S(1)}, u32[]{:S(2)}, u32[]{:S(2)}) collective-permute-start(bf16[1,4,4,256]{3,2,1,0:T(4,128)(2,1)S(1)} %slice_bitcast_fusion.10), channel_id=1, source_target_pairs={{1,0},{2,1},{3,2},{5,4},{6,5},{7,6},{9,8},{10,9},{11,10},{13,12},{... | collective-permute-start | bytes 24584 | tf_op jit(solution)/shard_map/ppermute | solution.py:25
  139.5 116.1 %collective-permute-start.14 = (bf16[64,512]{1,0:T(8,128)(2,1)S(1)}, bf16[64,512]{1,0:T(8,128)(2,1)S(1)}, u32[]{:S(2)}, u32[]{:S(2)}) collective-permute-start(bf16[64,512]{1,0:T(8,128)(2,1)S(1)} %bitcast_convert_fusion), channel_id=1, source_target_pairs={{0,4},{4,8},{8,12},{12,16},{16,20},{20,24},{24,28},{1,5},{5,9},{9,... | collective-permute-start | bytes 196616 | tf_op jit(solution)/shard_map/ppermute | solution.py:35
  155.2 4.7 %collective-permute-start.10 = (bf16[1,4,4,256]{3,2,1,0:T(4,128)(2,1)S(1)}, bf16[1,4,4,256]{3,2,1,0:T(4,128)(2,1)S(1)}, u32[]{:S(2)}, u32[]{:S(2)}) collective-permute-start(bf16[1,4,4,256]{3,2,1,0:T(4,128)(2,1)S(1)} %slice_bitcast_fusion.9), channel_id=1, source_target_pairs={{0,1},{1,2},{2,3},{4,5},{5,6},{6,7},{8,9},{9,10},{10,11},{12,13},{... | collective-permute-start | bytes 24584 | tf_op jit(solution)/shard_map/ppermute | solution.py:23
  158.0 4.1 %collective-permute-start.11 = (bf16[1,4,4,256]{3,2,1,0:T(4,128)(2,1)S(1)}, bf16[1,4,4,256]{3,2,1,0:T(4,128)(2,1)S(1)}, u32[]{:S(2)}, u32[]{:S(2)}) collective-permute-start(bf16[1,4,4,256]{3,2,1,0:T(4,128)(2,1)S(1)} %slice_bitcast_fusion.8), channel_id=1, source_target_pairs={{1,0},{2,1},{3,2},{5,4},{6,5},{7,6},{9,8},{10,9},{11,10},{13,12},{... | collective-permute-start | bytes 24584 | tf_op jit(solution)/shard_map/ppermute | solution.py:25
  174.4 8.8 %collective-permute-start.12 = (bf16[1,4,4,256]{3,2,1,0:T(4,128)(2,1)S(1)}, bf16[1,4,4,256]{3,2,1,0:T(4,128)(2,1)S(1)}, u32[]{:S(2)}, u32[]{:S(2)}) collective-permute-start(bf16[1,4,4,256]{3,2,1,0:T(4,128)(2,1)S(1)} %slice_bitcast_fusion.7), channel_id=1, source_target_pairs={{0,1},{1,2},{2,3},{4,5},{5,6},{6,7},{8,9},{9,10},{10,11},{12,13},{... | collective-permute-start | bytes 24584 | tf_op jit(solution)/shard_map/ppermute | solution.py:23
  178.7 4.5 %collective-permute-start.13 = (bf16[1,4,4,256]{3,2,1,0:T(4,128)(2,1)S(1)}, bf16[1,4,4,256]{3,2,1,0:T(4,128)(2,1)S(1)}, u32[]{:S(2)}, u32[]{:S(2)}) collective-permute-start(bf16[1,4,4,256]{3,2,1,0:T(4,128)(2,1)S(1)} %slice_bitcast_fusion.6), channel_id=1, source_target_pairs={{1,0},{2,1},{3,2},{5,4},{6,5},{7,6},{9,8},{10,9},{11,10},{13,12},{... | collective-permute-start | bytes 24584 | tf_op jit(solution)/shard_map/ppermute | solution.py:25
  194.8 5.1 %collective-permute-start.15 = (bf16[1,4,4,256]{3,2,1,0:T(4,128)(2,1)S(1)}, bf16[1,4,4,256]{3,2,1,0:T(4,128)(2,1)S(1)}, u32[]{:S(2)}, u32[]{:S(2)}) collective-permute-start(bf16[1,4,4,256]{3,2,1,0:T(4,128)(2,1)S(1)} %slice_bitcast_fusion.5), channel_id=1, source_target_pairs={{0,1},{1,2},{2,3},{4,5},{5,6},{6,7},{8,9},{9,10},{10,11},{12,13},{... | collective-permute-start | bytes 24584 | tf_op jit(solution)/shard_map/ppermute | solution.py:23
  197.9 3.8 %collective-permute-start.16 = (bf16[1,4,4,256]{3,2,1,0:T(4,128)(2,1)S(1)}, bf16[1,4,4,256]{3,2,1,0:T(4,128)(2,1)S(1)}, u32[]{:S(2)}, u32[]{:S(2)}) collective-permute-start(bf16[1,4,4,256]{3,2,1,0:T(4,128)(2,1)S(1)} %slice_bitcast_fusion.4), channel_id=1, source_target_pairs={{1,0},{2,1},{3,2},{5,4},{6,5},{7,6},{9,8},{10,9},{11,10},{13,12},{... | collective-permute-start | bytes 24584 | tf_op jit(solution)/shard_map/ppermute | solution.py:25
  253.7 9.3 %collective-permute-start.17 = (f32[64,512]{0,1:T(8,128)S(1)}, f32[64,512]{0,1:T(8,128)S(1)}, u32[]{:S(2)}, u32[]{:S(2)}) collective-permute-start(f32[64,512]{0,1:T(8,128)S(1)} %select_bitcast_fusion.1), channel_id=1, source_target_pairs={{4,0},{8,4},{12,8},{16,12},{20,16},{24,20},{28,24},{5,1},{9,5},{13... | collective-permute-start | bytes 393224 | tf_op jit(solution)/shard_map/ppermute | solution.py:35
where the time goes:
time: 269 us; the launch traced here: 265 us
  local copies, waits for them, and re-layouts  77.9 us (29%)
  other arithmetic  76 us (28%)
  starting transfers between devices  44.8 us (17%)
  blocking collectives  41.3 us (15%)
  waiting for transfers between devices  14.1 us (5%)
  between operations  11 us (4%)
    unnamed x15, other arithmetic  66.5 us
    psum x1, blocking collectives, per_device(): lax.psum(local_cost, ('tm', 'space'))  41.3 us
    ppermute x8, starting transfers between devices, padded_2(): lax.ppermute(tail, axis, [(i, (i + 1) % count) for i in range(ends)])  29.6 us
    gather x9, local copies, waits for them, and re-layouts, arrange(): return jnp.take(values, inverse, axis=-1)  29.1 us
    unnamed x24, local copies, waits for them, and re-layouts  18.2 us
    ppermute x8, starting transfers between devices, padded_2(): lax.ppermute(head, axis, [((i + 1) % count, i) for i in range(ends)])  10.5 us
    ppermute x8, waiting for transfers between devices, padded_2(): lax.ppermute(head, axis, [((i + 1) % count, i) for i in range(ends)])  8.76 us
    reshape x48, local copies, waits for them, and re-layouts, fetch(): return moved.reshape(traces.shape)  7.46 us
  transfers between devices with their start and end apart: 18, of which 6 were waited for; matrix products, arithmetic and copies ran while one was open for 35% of the time, Pallas kernels for 0%

commit v1 on v0

v1 whole, which is shorter than its diff:
```python
import functools

import jax
import jax.numpy as jnp
from jax import lax
from jax.experimental import pallas as pl
from jax.experimental.pallas import tpu as pltpu
from jax.sharding import PartitionSpec as P

NSIDE = 4
EXY = 16
BLOCK = NSIDE * NSIDE
HALF = 2 * BLOCK
LAYER = EXY * EXY
TIME_STEP = 0.1
PENALTY = 0.5
REGULAR = 0.1
F32 = jnp.float32
BF16 = jnp.bfloat16
RIM, MID = 0, 1
WIDE = 256


def dot(a, b):
    return jnp.dot(a, b, preferred_element_type=F32)


def rows_of(half):
    if half == RIM:
        return ((0, BLOCK), (3 * BLOCK, BLOCK))
    return ((BLOCK, BLOCK), (2 * BLOCK, BLOCK))


def take(ref, half, *lead):
    return jnp.concatenate([ref[lead + (slice(s, s + n),)] for s, n in rows_of(half)], axis=0)


def put(ref, half, value, *lead):
    at = 0
    for s, n in rows_of(half):
        ref[lead + (slice(s, s + n),)] = value[at : at + n]
        at += n


def fold(x):
    total = None
    for i in range(0, x.shape[0], 8):
        for j in range(0, x.shape[1], 128):
            piece = x[i : i + 8, j : j + 128]
            total = piece if total is None else total + piece
    return total


def lateral(x):
    rows, lanes = x.shape
    q = lax.broadcasted_iota(jnp.int32, x.shape, 0)
    s = lax.broadcasted_iota(jnp.int32, x.shape, 1)
    a, b = q % NSIDE, (q // NSIDE) % NSIDE
    col, row = s % EXY, (s // EXY) % EXY
    last = NSIDE - 1

    def along(which, node_step, place, lane_step):
        back = (EXY - 1) * lane_step
        low = which == 0
        z = jnp.where(low, pltpu.roll(x, rows - last * node_step, 0), pltpu.roll(x, last * node_step, 0))
        down = jnp.where(place == 0, pltpu.roll(z, lanes - back, 1), pltpu.roll(z, lane_step, 1))
        up = jnp.where(place == EXY - 1, pltpu.roll(z, back, 1), pltpu.roll(z, lanes - lane_step, 1))
        return jnp.where(low, down, jnp.where(which == last, up, 0.0))

    return along(a, 1, col, 1) + along(b, NSIDE, row, EXY)


def faces(half, shape):
    q = lax.broadcasted_iota(jnp.int32, shape, 0)
    a, b = q % NSIDE, (q // NSIDE) % NSIDE
    last = NSIDE - 1
    count = jnp.where((a == 0) | (a == last), 1.0, 0.0) + jnp.where((b == 0) | (b == last), 1.0, 0.0)
    return count + (1.0 if half == RIM else 0.0)


def kernel(
    n_space, n_tm,
    num_ref, ctl_hbm, tgt_hbm, st_hbm, adj_hbm, a_hbm,
    newc_ref, nst_ref, nadj_ref, obj_ref,
    a_ref, ctl, tgt, adj, st, hist, goal, r_ref, gf, pulled, part, xr, pa, pt,
    cost, rim_out, rim_in, st_out, st_in, adj_out, adj_in, slot_s, slot_t,
    in_sem, a_sem, rim_send, rim_recv, st_sem, adj_send_sem, adj_recv_sem,
    ss_send, ss_recv, tt_send, tt_recv,
):
    steps = ctl.shape[0]
    elements = ctl.shape[2]
    nodes = ctl.shape[1]
    me = lax.axis_index("space")
    t = lax.axis_index("tm")
    first = t * steps
    total_steps = steps * n_tm

    def weight(k):
        return (first + k).astype(F32) / total_steps

    loads = [
        pltpu.make_async_copy(src, dst, in_sem.at[i])
        for i, (src, dst) in enumerate(
            ((st_hbm.at[0], st), (ctl_hbm, ctl), (tgt_hbm, tgt), (adj_hbm.at[0], adj))
        )
    ]
    for c in loads:
        c.start()
    parts = a_sem.shape[0]
    chunk = nodes // parts
    a_loads = [
        pltpu.make_async_copy(a_hbm.at[pl.ds(i * chunk, chunk)], a_ref.at[pl.ds(i * chunk, chunk)], a_sem.at[i])
        for i in range(parts)
    ]
    for c in a_loads:
        c.start()

    rim_in[...] = jnp.zeros_like(rim_in)
    barrier = pltpu.get_barrier_semaphore()
    for d in range(1, n_space):
        pl.semaphore_signal(barrier, inc=1, device_id={"space": lax.rem(me + d, n_space)},
                            device_id_type=pl.DeviceIdType.MESH)
    for d in range(1, n_tm):
        pl.semaphore_signal(barrier, inc=1, device_id={"tm": lax.rem(t + d, n_tm)},
                            device_id_type=pl.DeviceIdType.MESH)

    for i in range(0, elements, WIDE):
        place = lax.broadcasted_iota(jnp.int32, (WIDE, elements), 0) + i
        hot = jnp.where(num_ref[...] == place, 1.0, 0.0)
        pt[i : i + WIDE, :] = hot.astype(BF16)
        pa[:, i : i + WIDE] = hot.T.astype(BF16)

    cost[...] = jnp.zeros_like(cost)

    def arrange(x):
        return dot(x.astype(BF16), pa[...])

    def restore(x):
        return dot(x.astype(BF16), pt[...])

    def rim_copy(rnd, side):
        peer = me - 1 if side == 0 else me + 1
        return pltpu.make_async_remote_copy(
            src_ref=rim_out.at[rnd, side], dst_ref=rim_in.at[rnd, 1 - side],
            send_sem=rim_send.at[rnd, side], recv_sem=rim_recv.at[rnd, 1 - side],
            device_id={"space": peer}, device_id_type=pl.DeviceIdType.MESH,
        )

    def send_rims(rnd, x):
        rim_out[rnd, 0] = x[:BLOCK, :LAYER].astype(BF16)
        rim_out[rnd, 1] = x[BLOCK:, elements - LAYER :].astype(BF16)

        @pl.when(me > 0)
        def _():
            rim_copy(rnd, 0).start()

        @pl.when(me < n_space - 1)
        def _():
            rim_copy(rnd, 1).start()

    def arrival(rnd, side):
        peer = me - 1 if side == 0 else me + 1
        return pltpu.make_async_remote_copy(
            src_ref=rim_out.at[rnd, side], dst_ref=rim_in.at[rnd, side],
            send_sem=rim_send.at[rnd, side], recv_sem=rim_recv.at[rnd, side],
            device_id={"space": peer}, device_id_type=pl.DeviceIdType.MESH,
        )

    def wait_rims(rnd):
        @pl.when(me > 0)
        def _():
            arrival(rnd, 0).wait()

        @pl.when(me < n_space - 1)
        def _():
            arrival(rnd, 1).wait()

    def rim_neighbours(rnd, x, lat):
        below = jnp.concatenate([rim_in[rnd, 0].astype(F32), x[BLOCK:, : elements - LAYER]], axis=1)
        above = jnp.concatenate([x[:BLOCK, LAYER:], rim_in[rnd, 1].astype(F32)], axis=1)
        return restore(lat + jnp.concatenate([below, above], axis=0))

    group = 8
    depth = group * HALF
    k_f = lax.broadcasted_iota(jnp.int32, (group, depth), 1) // HALF
    sum_rows = jnp.where(k_f == lax.broadcasted_iota(jnp.int32, (group, depth), 0), 1.0, 0.0).astype(BF16)
    k_b = lax.broadcasted_iota(jnp.int32, (HALF, depth), 1) % HALF
    sum_groups = jnp.where(k_b == lax.broadcasted_iota(jnp.int32, (HALF, depth), 0), 1.0, 0.0).astype(BF16)

    def groups_of(half):
        return [s + i for s, n in rows_of(half) for i in range(0, n, group)]

    def block_rows(i0, in_half, lanes):
        return jnp.concatenate(
            [a_ref[i0 : i0 + group, s : s + n, lanes] for s, n in rows_of(in_half)], axis=1
        )

    def apply(out_half, in_half, write):
        for n0 in range(0, elements, WIDE):
            lanes = slice(n0, n0 + WIDE)
            right = r_ref[in_half, :, lanes]
            for at, i0 in enumerate(groups_of(out_half)):
                q = (block_rows(i0, in_half, lanes) * right[None]).reshape(depth, WIDE)
                write(slice(at * group, (at + 1) * group), lanes, dot(sum_rows, q))

    def apply_t(out_half, in_half, write):
        for n0 in range(0, elements, WIDE):
            lanes = slice(n0, n0 + WIDE)
            acc = None
            for at, i0 in enumerate(groups_of(in_half)):
                pieces = []
                for i in range(group):
                    row = gf[in_half, at * group + i : at * group + i + 1, lanes]
                    spread = jnp.broadcast_to(row, (BLOCK, WIDE)).astype(BF16)
                    for s, n in rows_of(out_half):
                        pieces.append(a_ref[i0 + i, s : s + n, lanes] * spread)
                now = dot(sum_groups, jnp.concatenate(pieces, axis=0))
                acc = now if acc is None else acc + now
            write(lanes, acc)

    shape = (HALF, elements)

    def rhs(half, u, n, control):
        return (
            u + TIME_STEP * (u - u * u * u)
            + TIME_STEP * PENALTY * (n - faces(half, shape) * u)
            + TIME_STEP * control
        ).astype(BF16)

    loads[0].wait()
    for half in (RIM, MID):
        hist[0, half] = take(st, half)
    x0 = arrange(hist[0, RIM])
    xr[...] = x0
    pl.semaphore_wait(barrier, n_space - 1 + n_tm - 1)
    send_rims(0, x0)
    for c in loads[1:]:
        c.wait()
    for half in (RIM, MID):
        goal[half] = take(tgt, half).astype(F32)

    def forward(k, carry):
        um = hist[k, MID]
        nm = restore(lateral(arrange(um)))
        cm = take(ctl, MID, k).astype(F32)
        cr = take(ctl, RIM, k).astype(F32)
        r_ref[MID] = rhs(MID, um, nm, cm)
        x = xr[...]
        lat = lateral(x)

        @pl.when(k == 0)
        def _():
            for c in a_loads:
                c.wait()

        for out in (RIM, MID):
            def write(rows, lanes, v, out=out):
                hist[k + 1, out, rows, lanes] = v
            apply(out, MID, write)
        ur = hist[k, RIM]
        w = jnp.where(k > 0, weight(k), 0.0)
        dm, dr = um - goal[MID], ur - goal[RIM]
        cost[...] += 0.5 * w * fold(dm * dm + dr * dr) + 0.5 * REGULAR * fold(cm * cm + cr * cr)

        wait_rims(k)
        nr = rim_neighbours(k, x, lat)
        r_ref[RIM] = rhs(RIM, ur, nr, cr)

        def add(out):
            def write(rows, lanes, v):
                hist[k + 1, out, rows, lanes] += v
            return write

        apply(RIM, RIM, add(RIM))

        @pl.when(k < steps - 1)
        def _():
            y = arrange(hist[k + 1, RIM])
            xr[...] = y
            send_rims(k + 1, y)

        apply(MID, RIM, add(MID))
        return carry

    lax.fori_loop(0, steps, forward, 0)

    w_end = weight(steps)
    for half in (MID, RIM):
        u = hist[steps, half]
        d = u - goal[half]
        cost[...] += 0.5 * w_end * fold(d * d)
        gf[half] = w_end * d + take(adj, half)
        st_out[half] = u.astype(BF16)

    def st_copy(dst):
        return pltpu.make_async_remote_copy(
            src_ref=st_out, dst_ref=st_in, send_sem=st_sem.at[0], recv_sem=st_sem.at[1],
            device_id={"tm": dst}, device_id_type=pl.DeviceIdType.MESH)

    @pl.when(t < n_tm - 1)
    def _():
        st_copy(t + 1).start()

    slot_s[me] = cost[...]

    def gather_copy(slots, send, recv, axis, index, count, d):
        return pltpu.make_async_remote_copy(
            src_ref=slots.at[index], dst_ref=slots.at[index], send_sem=send.at[d], recv_sem=recv.at[index],
            device_id={axis: lax.rem(index + d, count)}, device_id_type=pl.DeviceIdType.MESH)

    def gather_wait(slots, send, recv, axis, index, count, d):
        gather_copy(slots, send, recv, axis, index, count, d).wait_send()
        origin = lax.rem(index + d, count)
        pltpu.make_async_remote_copy(
            src_ref=slots.at[origin], dst_ref=slots.at[origin], send_sem=send.at[d], recv_sem=recv.at[origin],
            device_id={axis: origin}, device_id_type=pl.DeviceIdType.MESH).wait_recv()

    over_s = (slot_s, ss_send, ss_recv, "space", me, n_space)
    over_t = (slot_t, tt_send, tt_recv, "tm", t, n_tm)
    for d in range(1, n_space):
        gather_copy(*over_s, d).start()

    def part_write(out):
        def write(lanes, v):
            part[out, :, lanes] = v
        return write

    def pulled_write(out):
        def write(lanes, v):
            pulled[out, :, lanes] = part[out, :, lanes] + v
        return write

    def finish(rnd):
        apply_t(RIM, RIM, pulled_write(RIM))
        y = arrange(pulled[RIM])
        xr[...] = y
        send_rims(rnd, y)
        apply_t(MID, RIM, pulled_write(MID))

    def carry_back(half, k, p, n):
        before = hist[k, half]
        carried = (
            p + TIME_STEP * (1.0 - 3.0 * before * before) * p
            + TIME_STEP * PENALTY * (n - faces(half, shape) * p)
        )
        return before, carried

    def update(half, k, p):
        control = take(ctl, half, k).astype(F32)
        put(newc_ref, half, (control - (TIME_STEP * p + REGULAR * control)).astype(BF16), k)

    apply_t(RIM, MID, part_write(RIM))
    apply_t(MID, MID, part_write(MID))
    finish(steps)

    def backward(i, carry):
        k = steps - 1 - i
        rnd = steps + i
        pm = pulled[MID]
        nm = restore(lateral(arrange(pm)))
        before, carried = carry_back(MID, k, pm, nm)
        gf[MID] = weight(k) * (before - goal[MID]) + carried
        x = xr[...]
        lat = lateral(x)
        apply_t(RIM, MID, part_write(RIM))
        apply_t(MID, MID, part_write(MID))
        pr = pulled[RIM]
        update(MID, k, pm)
        update(RIM, k, pr)

        @pl.when(i == 1)
        def _():
            for d in range(1, n_space):
                gather_wait(*over_s, d)
            total = slot_s[0]
            for j in range(1, n_space):
                total = total + slot_s[j]
            slot_t[t] = total
            for d in range(1, n_tm):
                gather_copy(*over_t, d).start()

        wait_rims(rnd)
        nr = rim_neighbours(rnd, x, lat)
        before_r, carried_r = carry_back(RIM, k, pr, nr)
        gf[RIM] = weight(k) * (before_r - goal[RIM]) + carried_r
        finish(rnd + 1)
        return carry

    lax.fori_loop(0, steps - 1, backward, 0)

    def adj_copy(dst, half):
        return pltpu.make_async_remote_copy(
            src_ref=adj_out.at[half], dst_ref=adj_in.at[half], send_sem=adj_send_sem.at[half],
            recv_sem=adj_recv_sem.at[half], device_id={"tm": dst}, device_id_type=pl.DeviceIdType.MESH)

    def send_adj(half, carried):
        adj_out[half] = carried.astype(adj_out.dtype)

        @pl.when(t > 0)
        def _():
            adj_copy(t - 1, half).start()

    rnd = 2 * steps - 1
    pm, pr = pulled[MID], pulled[RIM]
    nm = restore(lateral(arrange(pm)))
    send_adj(MID, carry_back(MID, 0, pm, nm)[1])
    x = xr[...]
    lat = lateral(x)
    wait_rims(rnd)
    nr = rim_neighbours(rnd, x, lat)
    send_adj(RIM, carry_back(RIM, 0, pr, nr)[1])
    update(MID, 0, pm)
    update(RIM, 0, pr)

    @pl.when(t == 0)
    def _():
        nst_ref[0] = st[...]

    @pl.when(t > 0)
    def _():
        st_copy(t - 1).wait_recv()
        for half in (RIM, MID):
            put(nst_ref, half, st_in[half].astype(F32), 0)

    @pl.when(t < n_tm - 1)
    def _():
        st_copy(t + 1).wait_send()

    for d in range(1, n_tm):
        gather_wait(*over_t, d)
    total = slot_t[0]
    for j in range(1, n_tm):
        total = total + slot_t[j]
    obj_ref[0, 0] = jnp.sum(total) * (1.0 / (total_steps * nodes * elements * n_space))

    @pl.when(t == n_tm - 1)
    def _():
        nadj_ref[...] = jnp.zeros_like(nadj_ref)

    @pl.when(t < n_tm - 1)
    def _():
        for half in (MID, RIM):
            adj_copy(t + 1, half).wait_recv()
            put(nadj_ref, half, adj_in[half].astype(F32), 0)

    @pl.when(t > 0)
    def _():
        for half in (MID, RIM):
            adj_copy(t - 1, half).wait_send()


def solution(mesh):
    n_space, n_tm = mesh.shape["space"], mesh.shape["tm"]

    def per_device(controls, target, state_in, adjoint_in, block_inverse, numbering):
        steps, nodes, elements = controls.shape
        vm = pl.BlockSpec(memory_space=pltpu.VMEM)
        anyspace = pl.BlockSpec(memory_space=pl.ANY)
        halves = (2, HALF, elements)
        rounds = 2 * steps
        dma = pltpu.SemaphoreType.DMA
        new_controls, next_state, next_adjoint, objective = pl.pallas_call(
            functools.partial(kernel, n_space, n_tm),
            out_shape=(
                jax.ShapeDtypeStruct(controls.shape, BF16),
                jax.ShapeDtypeStruct(state_in.shape, F32),
                jax.ShapeDtypeStruct(adjoint_in.shape, F32),
                jax.ShapeDtypeStruct((1, 1), F32),
            ),
            in_specs=[vm, anyspace, anyspace, anyspace, anyspace, anyspace],
            out_specs=(vm, vm, vm, pl.BlockSpec(memory_space=pltpu.SMEM)),
            scratch_shapes=[
                pltpu.VMEM(block_inverse.shape, BF16),
                pltpu.VMEM(controls.shape, BF16),
                pltpu.VMEM(target.shape, BF16),
                pltpu.VMEM(adjoint_in.shape[1:], F32),
                pltpu.VMEM(state_in.shape[1:], F32),
                pltpu.VMEM((steps + 1,) + halves, F32),
                pltpu.VMEM(halves, F32),
                pltpu.VMEM(halves, BF16),
                pltpu.VMEM(halves, F32),
                pltpu.VMEM(halves, F32),
                pltpu.VMEM(halves, F32),
                pltpu.VMEM(halves[1:], F32),
                pltpu.VMEM((elements, elements), BF16),
                pltpu.VMEM((elements, elements), BF16),
                pltpu.VMEM((8, 128), F32),
                pltpu.VMEM((rounds, 2, BLOCK, LAYER), BF16),
                pltpu.VMEM((rounds, 2, BLOCK, LAYER), BF16),
                pltpu.VMEM(halves, BF16),
                pltpu.VMEM(halves, BF16),
                pltpu.VMEM(halves, BF16),
                pltpu.VMEM(halves, BF16),
                pltpu.VMEM((n_space, 8, 128), F32),
                pltpu.VMEM((n_tm, 8, 128), F32),
                dma((4,)),
                dma((4,)),
                dma((rounds, 2)),
                dma((rounds, 2)),
                dma((2,)),
                dma((2,)),
                dma((2,)),
                dma((n_space,)),
                dma((n_space,)),
                dma((n_tm,)),
                dma((n_tm,)),
            ],
            compiler_params=pltpu.CompilerParams(
                collective_id=0, has_side_effects=True, vmem_limit_bytes=67043328
            ),
        )(numbering, controls, target, state_in, adjoint_in, block_inverse)
        return new_controls, next_state, next_adjoint, objective.reshape(())

    return jax.shard_map(
        per_device,
        mesh=mesh,
        in_specs=(
            P("tm", None, "space"),
            P(None, "space"),
            P("tm", None, "space"),
            P("tm", None, "space"),
            P(None, None, "space"),
            P("space", None),
        ),
        out_specs=(P("tm", None, "space"), P("tm", None, "space"), P("tm", None, "space"), P()),
        check_vma=False,
    )
```

time: 269 us -> 40.4 us (0.15); the launches traced: 265 us -> 40.2 us
  other arithmetic: 76 us -> 0 us
  local copies, waits for them, and re-layouts: 77.9 us -> 4.8 us
  starting transfers between devices: 44.8 us -> 0 us
  blocking collectives: 41.3 us -> 0 us
  Pallas kernels: 0 us -> 33.1 us
  waiting for transfers between devices: 14.1 us -> 0 us
  between operations: 11 us -> 2.34 us
    unnamed x15 -> x0, other arithmetic: 66.5 us -> none
    ppermute x18 -> x0, starting transfers between devices: 44.8 us -> none  [the longest x8 29.6 us: padded_2(): lax.ppermute(tail, axis, [(i, (i + 1) % count) for i in range(ends)])]
    psum x1 -> x0, blocking collectives: 41.3 us -> none  [per_device(): lax.psum(local_cost, ('tm', 'space'))]
    gather x12 -> x0, local copies, waits for them, and re-layouts: 33.3 us -> none  [the longest x9 29.1 us: arrange(): return jnp.take(values, inverse, axis=-1)]
    pallas_call x0 -> x1, Pallas kernels: none -> 33.1 us  [per_device(): pl.pallas_call(functools.partial(kernel, n_space, n_tm), out_shape=(jax.S...]
    ppermute x18 -> x0, waiting for transfers between devices: 14.1 us -> none  [the longest x8 8.76 us: padded_2(): lax.ppermute(head, axis, [((i + 1) % count, i) for i in range(ends)])]
    unnamed x24 -> x3, local copies, waits for them, and re-layouts: 18.2 us -> 4.8 us
    another operation x81 -> x0, local copies, waits for them, and re-layouts: 8.05 us -> none  [the longest x48 6.01 us: fetch(): shaped = traces.reshape(node_side, node_side, layers, EXY, EXY)]
  transfers between devices with their start and end apart: 18 -> 0, of which waited for: 6 -> 0; matrix products, arithmetic and copies ran while one was open for 35% -> 0% of each run, Pallas kernels for 0% -> 0%
where the time goes in v1:
time: 40.4 us; the launch traced here: 40.2 us
  Pallas kernels  33.1 us (82%)
  local copies, waits for them, and re-layouts  4.8 us (12%)
  between operations  2.34 us (6%)
    pallas_call x1, Pallas kernels, per_device(): pl.pallas_call(functools.partial(kernel, n_space, n_tm), out_shape=(jax.S...  33.1 us
    unnamed x3, local copies, waits for them, and re-layouts  4.8 us

profile of v1, /device:TPU:0, one launch (start us, length us, event | category | flops | bytes accessed | tf_op | source)
XLA Modules:
  0.0 40.2 jit_solution(3357693737160489029)
XLA Ops:
  0.6 33.1 %shard_map.93 = (bf16[4,64,512]{2,1,0:T(8,128)(2,1)}, f32[1,64,512]{2,1,0:T(8,128)}, f32[1,64,512]{2,1,0:T(8,128)}, f32[1,1]{1,0:T(1,128)}) custom-call(s32[1,512]{1,0:T(1,128)} %num_ref.1, bf16[4,64,512]{2,1,0:T(8,128)(2,1)} %ctl_hbm.1, bf16[64,512]{1,0:T(8,128)(2,1)} %tgt_hbm.1, f32[1,64,512]{2,1,0:T(8,128)} %st_hbm.1, f32[1,64,512]{2,1,0:T(8,128)} %adj_hbm.1, ...), custom_call_target="tpu_custom_call" | custom-call | tf_op jit(solution)/shard_map/pallas_call | solution.py:462
  33.7 1.7 %copy.14 = bf16[4,64,512]{2,1,0:T(8,128)(2,1)} copy(bf16[4,64,512]{2,1,0:T(8,128)(2,1)} %get-tuple-element.16) | data formatting | bytes 524288
  35.4 1.6 %copy.15 = f32[1,64,512]{2,1,0:T(8,128)} copy(f32[1,64,512]{2,1,0:T(8,128)} %get-tuple-element.17) | data formatting | bytes 262144
  37.0 1.6 %copy.16 = f32[1,64,512]{2,1,0:T(8,128)} copy(f32[1,64,512]{2,1,0:T(8,128)} %get-tuple-element.18) | data formatting | bytes 262144

commit v2 on v1

--- a/solution.py
+++ b/solution.py
@@ -449,13 +449,39 @@
             adj_copy(t - 1, half).wait_send()
 
 
+def store_kernel(count, *refs):
+    held = refs[2 * count : 3 * count]
+    sems = refs[-1]
+    takes = [pltpu.make_async_copy(refs[i], held[i], sems.at[0, i]) for i in range(count)]
+    gives = [pltpu.make_async_copy(held[i], refs[count + i], sems.at[1, i]) for i in range(count)]
+    for c in takes:
+        c.start()
+    for take_one, give in zip(takes, gives):
+        take_one.wait()
+        give.start()
+    for c in gives:
+        c.wait()
+
+
+def store(values):
+    count = len(values)
+    return pl.pallas_call(
+        functools.partial(store_kernel, count),
+        out_shape=tuple(jax.ShapeDtypeStruct(v.shape, v.dtype) for v in values),
+        in_specs=[pl.BlockSpec(memory_space=pltpu.HBM)] * count,
+        out_specs=(pl.BlockSpec(memory_space=pltpu.HBM),) * count,
+        scratch_shapes=[pltpu.VMEM(v.shape, v.dtype) for v in values] + [pltpu.SemaphoreType.DMA((2, count))],
+        compiler_params=pltpu.CompilerParams(vmem_limit_bytes=67043328),
+    )(*values)
+
+
 def solution(mesh):
     n_space, n_tm = mesh.shape["space"], mesh.shape["tm"]
 
     def per_device(controls, target, state_in, adjoint_in, block_inverse, numbering):
         steps, nodes, elements = controls.shape
         vm = pl.BlockSpec(memory_space=pltpu.VMEM)
-        anyspace = pl.BlockSpec(memory_space=pl.ANY)
+        hbm = pl.BlockSpec(memory_space=pltpu.HBM)
         halves = (2, HALF, elements)
         rounds = 2 * steps
         dma = pltpu.SemaphoreType.DMA
@@ -467,7 +493,7 @@
                 jax.ShapeDtypeStruct(adjoint_in.shape, F32),
                 jax.ShapeDtypeStruct((1, 1), F32),
             ),
-            in_specs=[vm, anyspace, anyspace, anyspace, anyspace, anyspace],
+            in_specs=[vm, hbm, hbm, hbm, hbm, hbm],
             out_specs=(vm, vm, vm, pl.BlockSpec(memory_space=pltpu.SMEM)),
             scratch_shapes=[
                 pltpu.VMEM(block_inverse.shape, BF16),
@@ -509,7 +535,7 @@
                 collective_id=0, has_side_effects=True, vmem_limit_bytes=67043328
             ),
         )(numbering, controls, target, state_in, adjoint_in, block_inverse)
-        return new_controls, next_state, next_adjoint, objective.reshape(())
+        return store((new_controls, next_state, next_adjoint)) + (objective.reshape(()),)
 
     return jax.shard_map(
         per_device,

time: 40.4 us -> 37.5 us (0.928)
  local copies, waits for them, and re-layouts: 4.8 us -> 0 us
  Pallas kernels: 33.1 us -> 34.9 us
    unnamed x3 -> x0, local copies, waits for them, and re-layouts: 4.8 us -> none
    pallas_call x0 -> x1, Pallas kernels: none -> 1.79 us  [store(): pl.pallas_call(functools.partial(store_kernel, count), out_shape=tuple((j...]
where the time goes in v2:
time: 37.5 us; the launch traced here: 37.3 us
  Pallas kernels  34.9 us (93%)
  between operations  2.41 us (6%)
    pallas_call x1, Pallas kernels, per_device(): pl.pallas_call(functools.partial(kernel, n_space, n_tm), out_shape=(jax.S...  33.1 us
    pallas_call x1, Pallas kernels, store(): pl.pallas_call(functools.partial(store_kernel, count), out_shape=tuple((j...  1.79 us

profile of v2, /device:TPU:0, one launch (start us, length us, event | category | flops | bytes accessed | tf_op | source)
XLA Modules:
  0.0 37.3 jit_solution(16708583511771608665)
XLA Ops:
  0.6 33.1 %shard_map.93 = (bf16[4,64,512]{2,1,0:T(8,128)(2,1)}, f32[1,64,512]{2,1,0:T(8,128)}, f32[1,64,512]{2,1,0:T(8,128)}, f32[1,1]{1,0:T(1,128)}) custom-call(s32[1,512]{1,0:T(1,128)} %num_ref.1, bf16[4,64,512]{2,1,0:T(8,128)(2,1)} %ctl_hbm.1, bf16[64,512]{1,0:T(8,128)(2,1)} %tgt_hbm.1, f32[1,64,512]{2,1,0:T(8,128)} %st_hbm.1, f32[1,64,512]{2,1,0:T(8,128)} %adj_hbm.1, ...), custom_call_target="tpu_custom_call" | custom-call | tf_op jit(solution)/shard_map/pallas_call | solution.py:488
  33.7 1.8 %shard_map.94 = (bf16[4,64,512]{2,1,0:T(8,128)(2,1)}, f32[1,64,512]{2,1,0:T(8,128)}, f32[1,64,512]{2,1,0:T(8,128)}) custom-call(bf16[4,64,512]{2,1,0:T(8,128)(2,1)} %get-tuple-element.11.refs_0_, f32[1,64,512]{2,1,0:T(8,128)} %get-tuple-element.12.refs_1_, f32[1,64,512]{2,1,0:T(8,128)} %get-tuple-element.13.refs_2_), custom_call_target="tpu_custom_call" | custom-call | tf_op jit(solution)/shard_map/pallas_call | solution.py:468
